TPU v7x, 32 devices: a whole 2x2x4 slice. The times are simulated.
32 devices in a mesh: atom: 8 (over z, x), aux: 4 (over y, core).
Axes of the slice: x: 2, y: 2, z: 4, core: 2. Of those that a mesh axis runs over, the one named last changes fastest.
Arguments:
- three_index: bfloat16 [128, 32, 128, 128], P('atom', 'aux'), may hold values from -6 to 6
- pair_mask: int32 [128, 8, 8], P('atom'), may hold values 0 or 1
- pair_owner: int32 [128, 1], P('atom'), may hold values from 0 to 7; in each aligned block of 16 rows (0 to 15, 16 to 31, ...) at most 2 rows name the same one
- pair_sub: int32 [128], P('atom'), may hold values from 0 to 3
- pair_nu: int32 [128], P('atom'), may hold values from 0 to 31
- live_count: int32 [8], P('atom'), may hold values from 1 to 16, 96 in all
- coefficients: bfloat16 [4096, 128], P('atom'), may hold values from -0.5 to 0.5
- fit_matrix: bfloat16 [32, 32], P('aux'), as said below
Outputs:
- exchange: float32 [4096, 4096], P('atom', 'aux')
Inputs may be any that keep to these rules, and one draw needn't show every extreme that they name: `pair_owner`: among the 16 slots of one atom index, at most 2 name the same owner, and in every draw some owner is named exactly 2 times by some atom index's slots. The first live_count[a] slots of atom index a are live; some atom index has all 16 slots live. `fit_matrix`: Symmetric.
All inputs are finite; a program needn't handle non-finite values. No bound on the sum of `pair_mask` or of `live_count` on one device may be relied on, other than what follows from the above.
Results may differ from a plain program's by a relative error of at most 0.012.
Values may be sent and summed in bfloat16 or wider, within the bound.
A program may use at most 128 MiB of HBM per device.

v0:
```python
import jax
import jax.numpy as jnp
from jax import lax
from jax.sharding import PartitionSpec as P

CAP = 2


def per_device(
    three_index, pair_mask, pair_owner, pair_sub, pair_nu, live_count, coefficients, fit_matrix
):
    slot_count, aux_here, block_size, _ = three_index.shape
    rows_here, occupied = coefficients.shape
    blocks_here = rows_here // block_size
    atom_count = lax.axis_size("atom")
    aux_total = fit_matrix.shape[1]
    basis_total = rows_here * atom_count
    shell_size = block_size // pair_mask.shape[1]
    whole_orbitals = lax.all_gather(coefficients, "atom", axis=0, tiled=True)
    orbital_blocks = whole_orbitals.reshape(basis_total // block_size, block_size, occupied)[
        pair_nu
    ]
    expanded = jnp.repeat(jnp.repeat(pair_mask, shell_size, 1), shell_size, 2).astype(jnp.bfloat16)
    masked = three_index * expanded[:, None, :, :]
    halfway = jnp.einsum(
        "tpmn,tni->tpim", masked, orbital_blocks, preferred_element_type=jnp.float32
    )
    alive_mask = jnp.arange(slot_count) < live_count[0]
    halfway = jnp.where(alive_mask[:, None, None, None], halfway, 0.0).astype(jnp.bfloat16)
    owners = pair_owner[:, 0]
    owner_hits = (owners[:, None] == jnp.arange(atom_count)[None, :]).astype(jnp.int32)
    rank_within = jnp.sum(jnp.cumsum(owner_hits, 0) * owner_hits, 1) - 1
    placement = owners * CAP + rank_within
    routing = (jnp.arange(atom_count * CAP)[:, None] == placement[None, :]).astype(jnp.bfloat16)
    outgoing = jnp.dot(routing, halfway.reshape(slot_count, -1), preferred_element_type=jnp.float32)
    outgoing = outgoing.astype(jnp.bfloat16).reshape(
        atom_count, CAP, aux_here, occupied, block_size
    )
    sub_codes = jnp.dot(
        routing, (pair_sub + 1).astype(jnp.bfloat16)[:, None], preferred_element_type=jnp.float32
    )
    sub_codes = sub_codes.astype(jnp.bfloat16).reshape(atom_count, CAP)
    arrived, arrived_codes = (
        lax.all_to_all(outgoing, "atom", split_axis=0, concat_axis=0, tiled=True),
        lax.all_to_all(sub_codes, "atom", split_axis=0, concat_axis=0, tiled=True),
    )
    wanted = (jnp.arange(blocks_here) + 1).astype(jnp.float32)
    selector = (arrived_codes.reshape(1, -1).astype(jnp.float32) == wanted[:, None]).astype(
        jnp.bfloat16
    )
    gathered_rows = jnp.einsum(
        "sc,cpib->pisb",
        selector,
        arrived.reshape(atom_count * CAP, aux_here, occupied, block_size),
        preferred_element_type=jnp.float32,
    )
    local_rows = gathered_rows.reshape(aux_here, occupied, rows_here).astype(jnp.bfloat16)
    fitted_sum = jnp.einsum(
        "qp,pir->qir",
        fit_matrix,
        lax.all_gather(local_rows, "aux", axis=0, tiled=True),
        preferred_element_type=jnp.float32,
    )
    fitted = fitted_sum.astype(jnp.bfloat16)
    partial_value = lax.dot_general(
        local_rows,
        lax.all_gather(fitted, "atom", axis=2, tiled=True),
        (((0, 1), (0, 1)), ((), ())),
        preferred_element_type=jnp.float32,
    )
    column_part = lax.psum_scatter(
        partial_value.astype(jnp.bfloat16), "aux", scatter_dimension=1, tiled=True
    ).astype(jnp.float32)
    return column_part * (aux_total * occupied) ** (-0.5)


def solution(mesh):
    in_specs = (
        P("atom", "aux", None, None),
        P("atom", None, None),
        P("atom", None),
        P("atom"),
        P("atom"),
        P("atom"),
        P("atom", None),
        P("aux", None),
    )
    out_specs = P("atom", "aux")
    return jax.shard_map(
        per_device, mesh=mesh, in_specs=in_specs, out_specs=out_specs, check_vma=False
    )
```

profile of v0, /device:TPU:5, one launch (start us, length us, event | category | flops | bytes accessed | tf_op | source)
XLA Modules:
  0.0 407.2 jit_solution(733651022336806653)
XLA Ops:
  6.5 0.7 all-gather.4.cloned.1.call-update
  7.3 0.7 fusion.25
  8.0 0.8 select_reduce_fusion
  8.9 0.7 add_add_fusion
  9.5 0.8 fusion.23
  10.3 0.7 all_to_all.12
  11.0 5.5 %all-to-all-start.1 = ((bf16[8,1,2]{2,1,0:T(2,128)(2,1)}), bf16[8,1,2]{2,1,0:T(2,128)(2,1)S(1)}, u32[]{:S(2)}, u32[]{:S(2)}) async-start(bf16[8,1,2]{2,1,0:T(2,128)(2,1)} %all_to_all.12), calls=%async_computation.1 | async-start | bytes 8192 | tf_op jit(solution)/shard_map/all_to_all | solution.py:45
  17.2 0.8 convert_element_type.76
  19.5 29.8 %all-gather.4.cloned.1.call-done = bf16[4096,128]{1,0:T(8,128)(2,1)} async-done(((bf16[512,128]{1,0:T(8,128)(2,1)}), bf16[4096,128]{1,0:T(8,128)(2,1)}) %all-gather.4.cloned.1.call-update) | async-done | bytes 1048592 | tf_op jit(solution)/shard_map/all_gather | solution.py:19
  49.3 1.9 gather_fusion
  51.1 4.1 select_convert_fusion
  55.2 2.5 fusion.12
  57.7 2.7 copy.31
  60.5 4.5 %all-to-all-start = ((bf16[8,2,8,128,128]{4,3,2,1,0:T(8,128)(2,1)}), bf16[8,2,8,128,128]{4,3,2,1,0:T(8,128)(2,1)}, u32[]{:S(2)}, u32[]{:S(2)}) async-start(bf16[8,2,8,128,128]{4,3,2,1,0:T(8,128)(2,1)} %bitcast.52), calls=%async_computation | async-start | bytes 8388608 | tf_op jit(solution)/shard_map/all_to_all | solution.py:44
  65.4 90.6 %all-to-all-done = bf16[8,2,8,128,128]{4,3,2,1,0:T(8,128)(2,1)} async-done(((bf16[8,2,8,128,128]{4,3,2,1,0:T(8,128)(2,1)}), bf16[8,2,8,128,128]{4,3,2,1,0:T(8,128)(2,1)}, u32[]{:S(2)}, u32[]{:S(2)}) %all-to-all-start) | async-done | bytes 4194336 | tf_op jit(solution)/shard_map/all_to_all | solution.py:44
  156.0 6.5 %copy.20 = bf16[8,2,8,128,128]{4,1,0,3,2:T(2,128)(2,1)S(1)} copy(bf16[8,2,8,128,128]{4,3,2,1,0:T(8,128)(2,1)} %all-to-all-done) | data formatting | bytes 8388608 | tf_op jit(solution)/shard_map/all_to_all | solution.py:44
  162.5 0.8 fusion.19
  163.3 1.2 convert_element_type.89
  164.6 35.4 %all-gather.6.cloned.1.call-done = bf16[32,128,512]{2,1,0:T(8,128)(2,1)} async-done(((bf16[8,128,512]{2,1,0:T(8,128)(2,1)}), bf16[32,128,512]{2,1,0:T(8,128)(2,1)}) %all-gather.6.cloned.1.call-update) | async-done | bytes 4194320 | tf_op jit(solution)/shard_map/all_gather | solution.py:61
  199.9 5.6 %fusion.20 = bf16[8,128,512]{2,0,1:T(8,128)(2,1)} fusion(bf16[32,128,512]{2,1,0:T(8,128)(2,1)} %all-gather.6.cloned.1.call-done, bf16[8,32]{1,0:T(8,128)(2,1)S(1)} %copy-done), kind=kOutput, calls=%fused_computation.18 | convolution fusion | flops 34078720 | bytes 5243392 | tf_op jit(solution)/shard_map/qp,pir->qir/dot_general | solution.py:58
  205.8 124.9 %all-gather.8.cloned.1.call-done = bf16[8,128,4096]{2,0,1:T(8,128)(2,1)} async-done(((bf16[8,128,512]{2,0,1:T(8,128)(2,1)}), bf16[8,128,4096]{2,0,1:T(8,128)(2,1)}) %all-gather.8.cloned.1.call-update) | async-done | bytes 8388624 | tf_op jit(solution)/shard_map/all_gather | solution.py:67
  330.7 24.8 %bitcast_convert_fusion = bf16[512,4096]{1,0:T(8,128)(2,1)} fusion(bf16[8,128,512]{2,1,0:T(8,128)(2,1)S(1)} %copy-done.1, bf16[8,128,4096]{2,0,1:T(8,128)(2,1)} %all-gather.8.cloned.1.call-done), kind=kOutput, calls=%fused_computation.2 | convolution fusion | flops 4297064448 | bytes 13631488 | tf_op jit(solution)/shard_map/dot_general | solution.py:65
  355.5 42.3 %reduce-scatter.2.cloned.1.call-done = bf16[512,1024]{1,0:T(8,128)(2,1)} async-done(((bf16[512,4096]{1,0:T(8,128)(2,1)}), bf16[512,1024]{1,0:T(8,128)(2,1)}) %reduce-scatter.2.cloned.1.call-update) | async-done | bytes 1048592 | tf_op jit(solution)/shard_map/reduce_scatter | solution.py:71
  397.9 2.8 convert_multiply_fusion
  (24 shorter events, 2.3 us)
Async XLA Ops:
  6.5 193.4 %copy-start = (bf16[8,32]{1,0:T(8,128)(2,1)S(1)}, bf16[8,32]{1,0:T(8,128)(2,1)}, u32[]{:S(2)}) copy-start(bf16[8,32]{1,0:T(8,128)(2,1)} %param.15) | copy-start | bytes 1540
  6.5 42.7 %all-gather.4.cloned.1.call-start = ((), (), s32[]{:S(2)}) async-start(), calls=%async_computation.3 | async-start | bytes 1179648 | tf_op jit(solution)/shard_map/all_gather | solution.py:19
  11.0 49.5 %all-to-all-start.1 = ((bf16[8,1,2]{2,1,0:T(2,128)(2,1)}), bf16[8,1,2]{2,1,0:T(2,128)(2,1)S(1)}, u32[]{:S(2)}, u32[]{:S(2)}) async-start(bf16[8,1,2]{2,1,0:T(2,128)(2,1)} %all_to_all.12), calls=%async_computation.1 | async-start | bytes 8192 | tf_op jit(solution)/shard_map/all_to_all | solution.py:45
  60.5 95.5 %all-to-all-start = ((bf16[8,2,8,128,128]{4,3,2,1,0:T(8,128)(2,1)}), bf16[8,2,8,128,128]{4,3,2,1,0:T(8,128)(2,1)}, u32[]{:S(2)}, u32[]{:S(2)}) async-start(bf16[8,2,8,128,128]{4,3,2,1,0:T(8,128)(2,1)} %bitcast.52), calls=%async_computation | async-start | bytes 8388608 | tf_op jit(solution)/shard_map/all_to_all | solution.py:44
  65.0 134.9 %all-gather.6.cloned.1.call-start = ((), (), s32[]{:S(2)}) async-start(), calls=%async_computation.4 | async-start | bytes 5242880 | tf_op jit(solution)/shard_map/all_gather | solution.py:61
  164.5 166.2 %copy-start.1 = (bf16[8,128,512]{2,1,0:T(8,128)(2,1)S(1)}, bf16[8,128,512]{2,1,0:T(8,128)(2,1)}, u32[]{:S(2)}) copy-start(bf16[8,128,512]{2,1,0:T(8,128)(2,1)} %convert_element_type.89) | copy-start | bytes 3145732
  164.5 166.2 %all-gather.8.cloned.1.call-start = ((), (), s32[]{:S(2)}) async-start(), calls=%async_computation.5 | async-start | bytes 9437184 | tf_op jit(solution)/shard_map/all_gather | solution.py:67
  205.6 192.3 %reduce-scatter.2.cloned.1.call-start = ((), (), s32[]{:S(2)}) async-start(), calls=%async_computation.6 | async-start | bytes 5242880 | tf_op jit(solution)/shard_map/reduce_scatter | solution.py:71
Sparse Core Ops, SparseCore 0:
  9.5 39.7 all-gather.3
  164.6 35.2 all-gather.5
  205.7 124.9 all-gather.7
  355.7 42.1 reduce-scatter.1
where the time goes:
time: 410 us; the launch traced here: 407 us
  waiting for transfers between devices  324 us (79%)
  matrix products  38.5 us (9%)
  local copies, waits for them, and re-layouts  14 us (3%)
  between operations  13.9 us (3%)
  starting transfers between devices  10.6 us (3%)
  other arithmetic  6.54 us (2%)
    all_gather x1, waiting for transfers between devices, per_device(): lax.all_gather(fitted, 'atom', axis=2, tiled=True)  125 us
    all_to_all x1, waiting for transfers between devices, per_device(): lax.all_to_all(outgoing, 'atom', split_axis=0, concat_axis=0, tiled=True)  90.6 us
    reduce_scatter x1, waiting for transfers between devices, per_device(): lax.psum_scatter(partial_value.astype(jnp.bfloat16), 'aux', scatter_dimen...  42.3 us
    all_gather x1, waiting for transfers between devices, per_device(): lax.all_gather(local_rows, 'aux', axis=0, tiled=True)  35.4 us
    all_gather x1, waiting for transfers between devices, per_device(): whole_orbitals = lax.all_gather(coefficients, 'atom', axis=0, tiled=True)  29.8 us
    dot_general x1, matrix products, per_device(): lax.dot_general(local_rows, lax.all_gather(fitted, 'atom', axis=2, tiled=...  24.8 us
  transfers between devices with their start and end apart: 6, of which 5 were waited for; matrix products, arithmetic and copies ran while one was open for 4% of the time, Pallas kernels for 0%

commit v1 on v0

--- a/solution.py
+++ b/solution.py
@@ -1,9 +1,273 @@
+import functools
+
 import jax
 import jax.numpy as jnp
 from jax import lax
+from jax.experimental import pallas as pl
+from jax.experimental.pallas import tpu as pltpu
 from jax.sharding import PartitionSpec as P
 
 CAP = 2
+MESH = pl.DeviceIdType.MESH
+
+
+def exchange_kernel(
+    atoms, auxes, h_ref, fit_ref, out_ref,
+    hall, hx, g, epart, cbuf, ybuf,
+    local_sem, sx, sz0, sz, rh, sa, ra, sc, rc, sy, ry,
+):
+    planes, ys = atoms // 2, auxes // 2
+    aux_here, rows, occ = h_ref.shape
+    me = lax.axis_index("atom")
+    ax = lax.axis_index("aux")
+    hi, lo = me // 2, me % 2
+    y, c = ax // 2, ax % 2
+    partner = {"atom": hi * 2 + 1 - lo, "aux": ax}
+    peer = {"atom": me, "aux": y * 2 + 1 - c}
+
+    barrier = pltpu.get_barrier_semaphore()
+
+    def greet(device):
+        pl.semaphore_signal(barrier, inc=1, device_id=device, device_id_type=MESH)
+
+    greet(partner)
+    greet(peer)
+    for d in range(1, ys):
+        greet({"atom": me, "aux": ((y + d) % ys) * 2 + c})
+
+    @pl.when(hi > 0)
+    def _():
+        greet({"atom": me - 2, "aux": ax})
+
+    @pl.when(hi < planes - 1)
+    def _():
+        greet({"atom": me + 2, "aux": ax})
+
+    before = jnp.minimum(hi, 1)
+    behind = jnp.minimum(planes - 1 - hi, 1)
+    pl.semaphore_wait(barrier, 1 + ys + before + behind)
+
+    def remote(src, dst, send, recv, device):
+        return pltpu.make_async_remote_copy(
+            src_ref=src, dst_ref=dst, send_sem=send, recv_sem=recv,
+            device_id=device, device_id_type=MESH,
+        )
+
+    def to_partner(k, atom, src):
+        return remote(src, hall.at[atom], sx.at[k], rh.at[atom], partner)
+
+    def along(atom, src, sem, step):
+        return remote(src, hall.at[atom], sem, rh.at[atom], {"atom": me + 2 * step, "aux": ax})
+
+    left_ok, right_ok = hi > 0, hi < planes - 1
+
+    @pl.when(left_ok)
+    def _():
+        along(me, h_ref, sz0.at[0], -1).start()
+
+    @pl.when(right_ok)
+    def _():
+        along(me, h_ref, sz0.at[1], 1).start()
+
+    to_partner(0, me, h_ref).start()
+    for d in range(1, ys):
+        remote(h_ref, hx.at[ax], sa.at[d], ra.at[ax], {"atom": me, "aux": ((y + d) % ys) * 2 + c}).start()
+    remote(h_ref, hx.at[ax], sa.at[0], ra.at[ax], peer).start()
+    own = pltpu.make_async_copy(h_ref, hall.at[me], local_sem.at[0])
+    own.start()
+    own_aux = pltpu.make_async_copy(h_ref, hx.at[ax], local_sem.at[1])
+    own_aux.start()
+
+    def plane_of(k):
+        half = (k + 1) // 2
+        return hi + half * (1 - 2 * (k % 2))
+
+    def valid(k):
+        p = plane_of(k)
+        return (p >= 0) & (p < planes) & (k < 2 * planes - 1)
+
+    def forward_ok(k):
+        target = hi - (1 - 2 * (k % 2))
+        return valid(k) & (target >= 0) & (target < planes)
+
+    def wait_block(atom):
+        remote(h_ref, hall.at[atom], sx.at[0], rh.at[atom], partner).wait_recv()
+
+    def relay(k):
+        @pl.when(valid(k))
+        def _():
+            atom = plane_of(k) * 2 + lo
+            wait_block(atom)
+
+            @pl.when(forward_ok(k))
+            def _():
+                along(atom, hall.at[atom], sz.at[k], -(1 - 2 * (k % 2))).start()
+
+            to_partner(k, atom, hall.at[atom]).start()
+
+    relay(1)
+    relay(2)
+
+    for d in range(1, ys):
+        src = ((y + d) % ys) * 2 + c
+        remote(h_ref, hx.at[src], sa.at[0], ra.at[src], peer).wait_recv()
+        remote(hx.at[src], hx.at[src], sa.at[ys - 1 + d], ra.at[src], peer).start()
+    for d in range(ys):
+        src = ((y + d) % ys) * 2 + 1 - c
+        remote(h_ref, hx.at[src], sa.at[0], ra.at[src], peer).wait_recv()
+    own_aux.wait()
+    own.wait()
+
+    piece = 32
+
+    @pl.loop(0, rows // piece)
+    def _(j):
+        at = pl.ds(pl.multiple_of(j * piece, piece), piece)
+        sums = [jnp.zeros((piece, occ), jnp.float32) for _ in range(aux_here)]
+        for p in range(aux_here * auxes):
+            block = hx[p // aux_here, p % aux_here, at, :].astype(jnp.float32)
+            for q in range(aux_here):
+                sums[q] = sums[q] + fit_ref[q, p] * block
+        for q in range(aux_here):
+            g[at, q * occ:(q + 1) * occ] = sums[q].astype(jnp.bfloat16)
+
+    width = 256
+
+    def product(k):
+        p = plane_of(k)
+
+        @pl.when(k > 0)
+        def _():
+            wait_block(p * 2 + 1 - lo)
+
+        @pl.when(k == 0)
+        def _():
+            wait_block(hi * 2 + 1 - lo)
+
+        for half in range(2):
+            @pl.loop(0, rows // width)
+            def _(j):
+                at = pl.ds(pl.multiple_of(j * width, width), width)
+                right = jnp.concatenate(
+                    [hall[p * 2 + half, q, at, :] for q in range(aux_here)], axis=-1
+                )
+                part = lax.dot_general(
+                    g[...], right, (((1,), (1,)), ((), ())), preferred_element_type=jnp.float32
+                )
+                col = pl.ds(pl.multiple_of(half * rows + j * width, width), width)
+                epart[p, :, col] = part.astype(jnp.bfloat16)
+
+        @pl.when(p % 2 != c)
+        def _():
+            remote(epart.at[p], cbuf.at[p // 2], sc.at[p // 2], rc.at[p // 2], peer).start()
+
+    def join(k):
+        p = plane_of(k)
+        yt = p // 2
+
+        @pl.when(p % 2 == c)
+        def _():
+            remote(epart.at[p], cbuf.at[yt], sc.at[yt], rc.at[yt], peer).wait_recv()
+
+            @pl.when(yt != y)
+            def _():
+                @pl.loop(0, rows // 64)
+                def _(j):
+                    at = pl.ds(pl.multiple_of(j * 64, 64), 64)
+                    total = epart[p, at, :].astype(jnp.float32) + cbuf[yt, at, :].astype(jnp.float32)
+                    epart[p, at, :] = total.astype(jnp.bfloat16)
+
+                remote(epart.at[p], ybuf.at[y], sy.at[yt], ry.at[y], {"atom": me, "aux": p}).start()
+
+    @pl.loop(0, 2 * planes)
+    def _(k):
+        @pl.when(valid(k))
+        def _():
+            product(k)
+
+        @pl.when(k > 0)
+        def _():
+            @pl.when(valid(k - 1))
+            def _():
+                join(k - 1)
+
+        relay(k + 3)
+
+    for d in range(1, ys):
+        src = (y + d) % ys
+        remote(epart.at[ax], ybuf.at[src], sy.at[src], ry.at[src], peer).wait_recv()
+
+    @pl.loop(0, rows // 64)
+    def _(j):
+        at = pl.ds(pl.multiple_of(j * 64, 64), 64)
+        total = epart[ax, at, :].astype(jnp.float32) + cbuf[y, at, :].astype(jnp.float32)
+        for d in range(1, ys):
+            total = total + ybuf[(y + d) % ys, at, :].astype(jnp.float32)
+        out_ref[at, :] = total
+
+    @pl.when(left_ok)
+    def _():
+        along(me, h_ref, sz0.at[0], -1).wait_send()
+
+    @pl.when(right_ok)
+    def _():
+        along(me, h_ref, sz0.at[1], 1).wait_send()
+
+    for k in range(2 * planes - 1):
+        @pl.when(valid(k))
+        def _():
+            to_partner(k, me, h_ref).wait_send()
+
+            if k > 0:
+                @pl.when(forward_ok(k))
+                def _():
+                    along(me, h_ref, sz.at[k], -(1 - 2 * (k % 2))).wait_send()
+
+    for d in range(2 * ys - 1):
+        remote(h_ref, hx.at[ax], sa.at[d], ra.at[ax], peer).wait_send()
+    for t in range(ys):
+        remote(epart.at[ax], cbuf.at[t], sc.at[t], rc.at[t], peer).wait_send()
+    for d in range(1, ys):
+        remote(epart.at[ax], ybuf.at[y], sy.at[(y + d) % ys], ry.at[y], peer).wait_send()
+
+
+def exchange_call(h, fit_rows):
+    aux_here, rows, occ = h.shape
+    atoms, auxes = lax.axis_size("atom"), lax.axis_size("aux")
+    planes, ys = atoms // 2, auxes // 2
+    columns = rows * atoms // auxes
+    dma = pltpu.SemaphoreType.DMA
+    return pl.pallas_call(
+        functools.partial(exchange_kernel, atoms, auxes),
+        out_shape=jax.ShapeDtypeStruct((rows, columns), jnp.float32),
+        in_specs=[
+            pl.BlockSpec(memory_space=pltpu.VMEM),
+            pl.BlockSpec(memory_space=pltpu.SMEM),
+        ],
+        out_specs=pl.BlockSpec(memory_space=pltpu.VMEM),
+        scratch_shapes=[
+            pltpu.VMEM((atoms, aux_here, rows, occ), jnp.bfloat16),
+            pltpu.VMEM((auxes, aux_here, rows, occ), jnp.bfloat16),
+            pltpu.VMEM((rows, aux_here * occ), jnp.bfloat16),
+            pltpu.VMEM((auxes, rows, columns), jnp.bfloat16),
+            pltpu.VMEM((ys, rows, columns), jnp.bfloat16),
+            pltpu.VMEM((ys, rows, columns), jnp.bfloat16),
+            dma((2,)),
+            dma((2 * planes - 1,)),
+            dma((2,)),
+            dma((2 * planes - 1,)),
+            dma((atoms,)),
+            dma((2 * ys - 1,)),
+            dma((auxes,)),
+            dma((ys,)),
+            dma((ys,)),
+            dma((ys,)),
+            dma((ys,)),
+        ],
+        compiler_params=pltpu.CompilerParams(
+            collective_id=0, has_side_effects=True, vmem_limit_bytes=60 * 1024 * 1024
+        ),
+    )(h, fit_rows)
 
 
 def per_device(
@@ -23,7 +287,7 @@
     expanded = jnp.repeat(jnp.repeat(pair_mask, shell_size, 1), shell_size, 2).astype(jnp.bfloat16)
     masked = three_index * expanded[:, None, :, :]
     halfway = jnp.einsum(
-        "tpmn,tni->tpim", masked, orbital_blocks, preferred_element_type=jnp.float32
+        "tpmn,tni->tpmi", masked, orbital_blocks, preferred_element_type=jnp.float32
     )
     alive_mask = jnp.arange(slot_count) < live_count[0]
     halfway = jnp.where(alive_mask[:, None, None, None], halfway, 0.0).astype(jnp.bfloat16)
@@ -34,7 +298,7 @@
     routing = (jnp.arange(atom_count * CAP)[:, None] == placement[None, :]).astype(jnp.bfloat16)
     outgoing = jnp.dot(routing, halfway.reshape(slot_count, -1), preferred_element_type=jnp.float32)
     outgoing = outgoing.astype(jnp.bfloat16).reshape(
-        atom_count, CAP, aux_here, occupied, block_size
+        atom_count, CAP, aux_here, block_size, occupied
     )
     sub_codes = jnp.dot(
         routing, (pair_sub + 1).astype(jnp.bfloat16)[:, None], preferred_element_type=jnp.float32
@@ -49,29 +313,14 @@
         jnp.bfloat16
     )
     gathered_rows = jnp.einsum(
-        "sc,cpib->pisb",
+        "sc,cpmi->psmi",
         selector,
-        arrived.reshape(atom_count * CAP, aux_here, occupied, block_size),
+        arrived.reshape(atom_count * CAP, aux_here, block_size, occupied),
         preferred_element_type=jnp.float32,
     )
-    local_rows = gathered_rows.reshape(aux_here, occupied, rows_here).astype(jnp.bfloat16)
-    fitted_sum = jnp.einsum(
-        "qp,pir->qir",
-        fit_matrix,
-        lax.all_gather(local_rows, "aux", axis=0, tiled=True),
-        preferred_element_type=jnp.float32,
-    )
-    fitted = fitted_sum.astype(jnp.bfloat16)
-    partial_value = lax.dot_general(
-        local_rows,
-        lax.all_gather(fitted, "atom", axis=2, tiled=True),
-        (((0, 1), (0, 1)), ((), ())),
-        preferred_element_type=jnp.float32,
-    )
-    column_part = lax.psum_scatter(
-        partial_value.astype(jnp.bfloat16), "aux", scatter_dimension=1, tiled=True
-    ).astype(jnp.float32)
-    return column_part * (aux_total * occupied) ** (-0.5)
+    local_rows = gathered_rows.reshape(aux_here, rows_here, occupied).astype(jnp.bfloat16)
+    total = exchange_call(local_rows, fit_matrix.astype(jnp.float32))
+    return total * (aux_total * occupied) ** (-0.5)
 
 
 def solution(mesh):

time: 410 us -> 292 us (0.71)
  waiting for transfers between devices: 324 us -> 121 us
  Pallas kernels: 0 us -> 117 us
  matrix products: 38.5 us -> 7.48 us
    all_gather x2 -> x0, waiting for transfers between devices: 160 us -> none  [the longest x1 125 us: per_device(): lax.all_gather(fitted, 'atom', axis=2, tiled=True)]
    pallas_call x0 -> x1, Pallas kernels: none -> 117 us  [exchange_call(): pl.pallas_call(functools.partial(exchange_kernel, atoms, auxes), out_shap...]
    reduce_scatter x1 -> x0, waiting for transfers between devices: 42.3 us -> none  [per_device(): lax.psum_scatter(partial_value.astype(jnp.bfloat16), 'aux', scatter_dimen...]
    dot_general x4 -> x2, matrix products: 35.2 us -> 4.18 us  [the longest x1 3.43 us: per_device(): jnp.einsum('tpmn,tni->tpmi', masked, orbital_blocks, preferred_element_ty...]
  transfers between devices with their start and end apart: 6 -> 3, of which waited for: 5 -> 2; matrix products, arithmetic and copies ran while one was open for 4% -> 6% of each run, Pallas kernels for 0% -> 0%
where the time goes in v1:
time: 292 us; the launch traced here: 291 us
  waiting for transfers between devices  121 us (41%)
  Pallas kernels  117 us (40%)
  between operations  14.2 us (5%)
  local copies, waits for them, and re-layouts  14 us (5%)
  starting transfers between devices  10.2 us (3%)
  other arithmetic  7.53 us (3%)
  matrix products  7.48 us (3%)
    pallas_call x1, Pallas kernels, exchange_call(): pl.pallas_call(functools.partial(exchange_kernel, atoms, auxes), out_shap...  117 us
    all_to_all x1, waiting for transfers between devices, per_device(): lax.all_to_all(outgoing, 'atom', split_axis=0, concat_axis=0, tiled=True)  90.2 us
    all_gather x1, waiting for transfers between devices, per_device(): whole_orbitals = lax.all_gather(coefficients, 'atom', axis=0, tiled=True)  29.8 us
    all_to_all x1, local copies, waits for them, and re-layouts, per_device(): lax.all_to_all(outgoing, 'atom', split_axis=0, concat_axis=0, tiled=True)  6.5 us
  transfers between devices with their start and end apart: 3, of which 2 were waited for; matrix products, arithmetic and copies ran while one was open for 6% of the time, Pallas kernels for 0%

profile of v1, /device:TPU:5, one launch (start us, length us, event | category | flops | bytes accessed | tf_op | source)
XLA Modules:
  0.0 291.2 jit_solution(12250101173852913495)
XLA Ops:
  6.5 0.7 all-gather.2.cloned.1.call-update
  7.3 0.7 fusion.13
  8.0 0.8 select_reduce_fusion
  8.9 0.7 add_add_fusion
  9.5 0.8 fusion.11
  10.3 0.7 all_to_all.12
  11.0 5.5 %all-to-all-start.1 = ((bf16[8,1,2]{2,1,0:T(2,128)(2,1)}), bf16[8,1,2]{2,1,0:T(2,128)(2,1)S(1)}, u32[]{:S(2)}, u32[]{:S(2)}) async-start(bf16[8,1,2]{2,1,0:T(2,128)(2,1)} %all_to_all.12), calls=%async_computation.1 | async-start | bytes 8192 | tf_op jit(solution)/shard_map/all_to_all | solution.py:309
  16.5 0.8 convert_element_type.62
  17.4 0.2 broadcast_in_dim.29
  17.9 0.3 copy.17
  18.8 0.7 compare_select_fusion
  19.5 29.8 %all-gather.2.cloned.1.call-done = bf16[4096,128]{1,0:T(8,128)(2,1)} async-done(((bf16[512,128]{1,0:T(8,128)(2,1)}), bf16[4096,128]{1,0:T(8,128)(2,1)}) %all-gather.2.cloned.1.call-update) | async-done | bytes 1048592 | tf_op jit(solution)/shard_map/all_gather | solution.py:283
  49.3 1.9 gather_fusion
  51.1 3.4 %select_convert_fusion = bf16[16,8,128,128]{3,2,1,0:T(8,128)(2,1)S(1)} fusion(pred[16]{0:T(512)(128)(4,1)S(1)} %iota_compare_fusion.4, bf16[16,8,128,128]{3,2,1,0:T(8,128)(2,1)} %param.8, bf16[16,128,128]{2,1,0:T(8,128)(2,1)S(1)} %copy.17, bf16[16,128,128]{2,1,0:T(8,128)(2,1)S(1)} %gather_fusion), kind=kOutput, calls=%fused_computation.2 | convolution fusion | flops 543162368 | bytes 9437200 | tf_op jit(solution)/shard_map/tpmn,tni->tpmi/dot_general | solution.py:289
  54.6 2.5 fusion.6
  57.1 2.7 copy.24
  59.9 4.7 %all-to-all-start = ((bf16[8,2,8,128,128]{4,3,2,1,0:T(8,128)(2,1)}), bf16[8,2,8,128,128]{4,3,2,1,0:T(8,128)(2,1)}, u32[]{:S(2)}, u32[]{:S(2)}) async-start(bf16[8,2,8,128,128]{4,3,2,1,0:T(8,128)(2,1)} %bitcast.44), calls=%async_computation | async-start | bytes 8388608 | tf_op jit(solution)/shard_map/all_to_all | solution.py:308
  64.6 0.6 convert_element_type.75.fit_ref
  65.2 90.2 %all-to-all-done = bf16[8,2,8,128,128]{4,3,2,1,0:T(8,128)(2,1)} async-done(((bf16[8,2,8,128,128]{4,3,2,1,0:T(8,128)(2,1)}), bf16[8,2,8,128,128]{4,3,2,1,0:T(8,128)(2,1)}, u32[]{:S(2)}, u32[]{:S(2)}) %all-to-all-start) | async-done | bytes 4194336 | tf_op jit(solution)/shard_map/all_to_all | solution.py:308
  155.5 6.5 %copy.18 = bf16[8,2,8,128,128]{4,1,0,3,2:T(2,128)(2,1)S(1)} copy(bf16[8,2,8,128,128]{4,3,2,1,0:T(8,128)(2,1)} %all-to-all-done) | data formatting | bytes 8388608 | tf_op jit(solution)/shard_map/all_to_all | solution.py:308
  162.0 0.8 fusion.10
  162.8 1.2 copy.20
  164.0 117.1 %shard_map.82 = f32[512,1024]{1,0:T(8,128)} custom-call(bf16[8,512,128]{2,1,0:T(8,128)(2,1)} %bitcast.46, f32[8,32]{1,0:T(8,128)} %convert_element_type.75.fit_ref), custom_call_target="tpu_custom_call" | custom-call | tf_op jit(solution)/shard_map/pallas_call | solution.py:240
  281.1 3.2 %broadcast_multiply_fusion = f32[512,1024]{1,0:T(8,128)} fusion(f32[512,1024]{1,0:T(8,128)} %shard_map.82), kind=kLoop, calls=%fused_computation.13 | loop fusion | flops 524288 | bytes 4194304 | tf_op jit(solution)/shard_map/mul | solution.py:323
  (13 shorter events, 0.5 us)
Async XLA Ops:
  6.5 42.7 %all-gather.2.cloned.1.call-start = ((), (), s32[]{:S(2)}) async-start(), calls=%async_computation.2 | async-start | bytes 1179648 | tf_op jit(solution)/shard_map/all_gather | solution.py:283
  11.0 48.9 %all-to-all-start.1 = ((bf16[8,1,2]{2,1,0:T(2,128)(2,1)}), bf16[8,1,2]{2,1,0:T(2,128)(2,1)S(1)}, u32[]{:S(2)}, u32[]{:S(2)}) async-start(bf16[8,1,2]{2,1,0:T(2,128)(2,1)} %all_to_all.12), calls=%async_computation.1 | async-start | bytes 8192 | tf_op jit(solution)/shard_map/all_to_all | solution.py:309
  59.9 4.7 %copy-start = (bf16[8,32]{1,0:T(8,128)(2,1)S(1)}, bf16[8,32]{1,0:T(8,128)(2,1)}, u32[]{:S(2)}) copy-start(bf16[8,32]{1,0:T(8,128)(2,1)} %param.15) | copy-start | bytes 1540
  59.9 95.6 %all-to-all-start = ((bf16[8,2,8,128,128]{4,3,2,1,0:T(8,128)(2,1)}), bf16[8,2,8,128,128]{4,3,2,1,0:T(8,128)(2,1)}, u32[]{:S(2)}, u32[]{:S(2)}) async-start(bf16[8,2,8,128,128]{4,3,2,1,0:T(8,128)(2,1)} %bitcast.44), calls=%async_computation | async-start | bytes 8388608 | tf_op jit(solution)/shard_map/all_to_all | solution.py:308
Sparse Core Ops, SparseCore 0:
  9.5 39.7 all-gather.1

commit v2 on v1

--- a/solution.py
+++ b/solution.py
@@ -270,55 +270,255 @@
     )(h, fit_rows)
 
 
+def route_kernel(
+    atoms, order_ref, nu_ref, three_ref, mask_ref, code_ref, own_ref, out_ref,
+    orbitals, outgoing, arrived, codes, acc,
+    local_sem, sx, sz0, sz, rh, sd, rd, sk, rk,
+):
+    planes, middle = atoms // 2, atoms // 2
+    cap = code_ref.shape[1]
+    per, size, occ = own_ref.shape
+    aux_here = three_ref.shape[1]
+    me = lax.axis_index("atom")
+    ax = lax.axis_index("aux")
+    hi, lo = me // 2, me % 2
+    side, pos = me // middle, me % middle
+
+    def at_atom(atom):
+        return {"atom": atom, "aux": ax}
+
+    barrier = pltpu.get_barrier_semaphore()
+    for d in range(1, atoms):
+        pl.semaphore_signal(
+            barrier, inc=1, device_id=at_atom((me + d) % atoms), device_id_type=MESH
+        )
+    pl.semaphore_wait(barrier, atoms - 1)
+
+    def remote(src, dst, send, recv, device):
+        return pltpu.make_async_remote_copy(
+            src_ref=src, dst_ref=dst, send_sem=send, recv_sem=recv,
+            device_id=device, device_id_type=MESH,
+        )
+
+    def spot(atom):
+        return orbitals.at[pl.ds(atom * per, per)]
+
+    def to_partner(k, atom, src):
+        return remote(src, spot(atom), sx.at[k], rh.at[atom], at_atom(hi * 2 + 1 - lo))
+
+    def along(atom, src, sem, step):
+        return remote(src, spot(atom), sem, rh.at[atom], at_atom(me + 2 * step))
+
+    left_ok, right_ok = hi > 0, hi < planes - 1
+
+    @pl.when(left_ok)
+    def _():
+        along(me, own_ref, sz0.at[0], -1).start()
+
+    @pl.when(right_ok)
+    def _():
+        along(me, own_ref, sz0.at[1], 1).start()
+
+    to_partner(0, me, own_ref).start()
+    own = pltpu.make_async_copy(own_ref, spot(me), local_sem.at[0])
+    own.start()
+
+    def plane_of(k):
+        half = (k + 1) // 2
+        return hi + half * (1 - 2 * (k % 2))
+
+    def valid(k):
+        p = plane_of(k)
+        return (p >= 0) & (p < planes)
+
+    def forward_ok(k):
+        target = hi - (1 - 2 * (k % 2))
+        return valid(k) & (target >= 0) & (target < planes)
+
+    def wait_block(atom):
+        remote(own_ref, spot(atom), sx.at[0], rh.at[atom], at_atom(hi * 2 + 1 - lo)).wait_recv()
+
+    @pl.loop(1, 2 * planes - 1)
+    def _(k):
+        @pl.when(valid(k))
+        def _():
+            atom = plane_of(k) * 2 + lo
+            wait_block(atom)
+
+            @pl.when(forward_ok(k))
+            def _():
+                along(atom, spot(atom), sz.at[k], -(1 - 2 * (k % 2))).start()
+
+            to_partner(k, atom, spot(atom)).start()
+
+    @pl.loop(0, planes)
+    def _(p):
+        wait_block(p * 2 + 1 - lo)
+
+    own.wait()
+
+    def half_block(place):
+        slot, nu = order_ref[place], nu_ref[place]
+        right = orbitals[nu]
+        left = three_ref[slot] * mask_ref[slot][None, :, :]
+        value = jnp.dot(
+            left.reshape(aux_here * size, size), right, preferred_element_type=jnp.float32
+        )
+        return value.reshape(aux_here, size, occ).astype(jnp.bfloat16)
+
+    def target_of(j):
+        far = (1 - side) * middle + (pos + j) % middle
+        near = side * middle + (pos + j + 1) % middle
+        return jnp.where(j < middle, far, near)
+
+    @pl.loop(0, atoms - 1)
+    def _(j):
+        target = target_of(j)
+
+        @pl.loop(0, cap)
+        def _(r):
+            outgoing[j, r] = half_block(target * cap + r)
+
+        remote(outgoing.at[j], arrived.at[me], sd.at[j], rd.at[me], at_atom(target)).start()
+        remote(code_ref.at[target], codes.at[me], sk.at[j], rk.at[me], at_atom(target)).start()
+
+    @pl.loop(0, cap)
+    def _(r):
+        arrived[me, r] = half_block(me * cap + r)
+
+    keep = pltpu.make_async_copy(code_ref.at[me], codes.at[me], local_sem.at[1])
+    keep.start()
+    keep.wait()
+    acc[...] = jnp.zeros_like(acc)
+
+    def take(src):
+        hits = [
+            [codes[src, r, b] for r in range(cap)]
+            for b in range(per)
+        ]
+
+        @pl.loop(0, aux_here * (size // 64))
+        def _(n):
+            p, part = n // (size // 64), n % (size // 64)
+            at = pl.ds(pl.multiple_of(part * 64, 64), 64)
+            values = [
+                arrived[src, r, p, at, :].astype(jnp.float32).reshape(8, 8, occ)
+                for r in range(cap)
+            ]
+            for b in range(per):
+                to = pl.ds(pl.multiple_of(b * size + part * 64, 64), 64)
+                total = acc[p, to, :].reshape(8, 8, occ)
+                for r in range(cap):
+                    total = total + values[r] * hits[b][r][None]
+                acc[p, to, :] = total.reshape(64, occ)
+
+    take(me)
+
+    @pl.loop(0, atoms - 1)
+    def _(j):
+        near = side * middle + (pos + j + 1) % middle
+        far = (1 - side) * middle + (pos + 2 * middle - 1 - j) % middle
+        src = jnp.where(j < middle - 1, near, far)
+        remote(outgoing.at[0], arrived.at[src], sd.at[0], rd.at[src], at_atom(src)).wait_recv()
+        remote(code_ref.at[0], codes.at[src], sk.at[0], rk.at[src], at_atom(src)).wait_recv()
+        take(src)
+
+    out_ref[...] = acc[...].astype(jnp.bfloat16)
+
+    @pl.when(left_ok)
+    def _():
+        along(me, own_ref, sz0.at[0], -1).wait_send()
+
+    @pl.when(right_ok)
+    def _():
+        along(me, own_ref, sz0.at[1], 1).wait_send()
+
+    to_partner(0, me, own_ref).wait_send()
+
+    @pl.loop(1, 2 * planes - 1)
+    def _(k):
+        @pl.when(valid(k))
+        def _():
+            to_partner(k, me, own_ref).wait_send()
+
+            @pl.when(forward_ok(k))
+            def _():
+                along(me, own_ref, sz.at[k], -(1 - 2 * (k % 2))).wait_send()
+
+    @pl.loop(0, atoms - 1)
+    def _(j):
+        target = target_of(j)
+        remote(outgoing.at[j], arrived.at[me], sd.at[j], rd.at[me], at_atom(target)).wait_send()
+        remote(code_ref.at[target], codes.at[me], sk.at[j], rk.at[me], at_atom(target)).wait_send()
+
+
+def route_call(order, nu, three_index, mask, codes, coefficients):
+    aux_here, size = three_index.shape[1], three_index.shape[2]
+    rows, occ = coefficients.shape
+    per = rows // size
+    atoms = lax.axis_size("atom")
+    planes = atoms // 2
+    dma = pltpu.SemaphoreType.DMA
+    smem = pl.BlockSpec(memory_space=pltpu.SMEM)
+    vmem = pl.BlockSpec(memory_space=pltpu.VMEM)
+    return pl.pallas_call(
+        functools.partial(route_kernel, atoms),
+        out_shape=jax.ShapeDtypeStruct((aux_here, rows, occ), jnp.bfloat16),
+        in_specs=[smem, smem, vmem, vmem, vmem, vmem],
+        out_specs=vmem,
+        scratch_shapes=[
+            pltpu.VMEM((atoms * per, size, occ), jnp.bfloat16),
+            pltpu.VMEM((atoms - 1, CAP, aux_here, size, occ), jnp.bfloat16),
+            pltpu.VMEM((atoms, CAP, aux_here, size, occ), jnp.bfloat16),
+            pltpu.VMEM((atoms, CAP, per, 8, 128), jnp.float32),
+            pltpu.VMEM((aux_here, rows, occ), jnp.float32),
+            dma((2,)),
+            dma((2 * planes - 1,)),
+            dma((2,)),
+            dma((2 * planes - 1,)),
+            dma((atoms,)),
+            dma((atoms - 1,)),
+            dma((atoms,)),
+            dma((atoms - 1,)),
+            dma((atoms,)),
+        ],
+        compiler_params=pltpu.CompilerParams(
+            collective_id=1, has_side_effects=True, vmem_limit_bytes=60 * 1024 * 1024
+        ),
+    )(order, nu, three_index, mask, codes, coefficients.reshape(per, size, occ))
+
+
 def per_device(
     three_index, pair_mask, pair_owner, pair_sub, pair_nu, live_count, coefficients, fit_matrix
 ):
     slot_count, aux_here, block_size, _ = three_index.shape
     rows_here, occupied = coefficients.shape
-    blocks_here = rows_here // block_size
     atom_count = lax.axis_size("atom")
     aux_total = fit_matrix.shape[1]
-    basis_total = rows_here * atom_count
     shell_size = block_size // pair_mask.shape[1]
-    whole_orbitals = lax.all_gather(coefficients, "atom", axis=0, tiled=True)
-    orbital_blocks = whole_orbitals.reshape(basis_total // block_size, block_size, occupied)[
-        pair_nu
-    ]
     expanded = jnp.repeat(jnp.repeat(pair_mask, shell_size, 1), shell_size, 2).astype(jnp.bfloat16)
-    masked = three_index * expanded[:, None, :, :]
-    halfway = jnp.einsum(
-        "tpmn,tni->tpmi", masked, orbital_blocks, preferred_element_type=jnp.float32
-    )
-    alive_mask = jnp.arange(slot_count) < live_count[0]
-    halfway = jnp.where(alive_mask[:, None, None, None], halfway, 0.0).astype(jnp.bfloat16)
     owners = pair_owner[:, 0]
     owner_hits = (owners[:, None] == jnp.arange(atom_count)[None, :]).astype(jnp.int32)
     rank_within = jnp.sum(jnp.cumsum(owner_hits, 0) * owner_hits, 1) - 1
     placement = owners * CAP + rank_within
-    routing = (jnp.arange(atom_count * CAP)[:, None] == placement[None, :]).astype(jnp.bfloat16)
-    outgoing = jnp.dot(routing, halfway.reshape(slot_count, -1), preferred_element_type=jnp.float32)
-    outgoing = outgoing.astype(jnp.bfloat16).reshape(
-        atom_count, CAP, aux_here, block_size, occupied
+    routing = (jnp.arange(atom_count * CAP)[:, None] == placement[None, :]).astype(jnp.int32)
+    slots = jnp.arange(slot_count, dtype=jnp.int32)
+
+    def placed(values):
+        return jnp.sum(routing * values[None, :], 1)
+
+    live_codes = placed(jnp.where(slots < live_count[0], pair_sub + 1, 0))
+    blocks = jnp.arange(rows_here // block_size)
+    hits = (live_codes[:, None] == blocks[None, :] + 1).astype(jnp.float32)
+    hits = hits.reshape(atom_count, CAP, blocks.shape[0], 1, 1)
+    local_rows = route_call(
+        placed(slots),
+        placed(pair_nu),
+        three_index,
+        expanded,
+        jnp.broadcast_to(hits, hits.shape[:3] + (8, 128)),
+        coefficients,
     )
-    sub_codes = jnp.dot(
-        routing, (pair_sub + 1).astype(jnp.bfloat16)[:, None], preferred_element_type=jnp.float32
-    )
-    sub_codes = sub_codes.astype(jnp.bfloat16).reshape(atom_count, CAP)
-    arrived, arrived_codes = (
-        lax.all_to_all(outgoing, "atom", split_axis=0, concat_axis=0, tiled=True),
-        lax.all_to_all(sub_codes, "atom", split_axis=0, concat_axis=0, tiled=True),
-    )
-    wanted = (jnp.arange(blocks_here) + 1).astype(jnp.float32)
-    selector = (arrived_codes.reshape(1, -1).astype(jnp.float32) == wanted[:, None]).astype(
-        jnp.bfloat16
-    )
-    gathered_rows = jnp.einsum(
-        "sc,cpmi->psmi",
-        selector,
-        arrived.reshape(atom_count * CAP, aux_here, block_size, occupied),
-        preferred_element_type=jnp.float32,
-    )
-    local_rows = gathered_rows.reshape(aux_here, rows_here, occupied).astype(jnp.bfloat16)
     total = exchange_call(local_rows, fit_matrix.astype(jnp.float32))
     return total * (aux_total * occupied) ** (-0.5)
 

time: 292 us -> 248 us (0.85)
  waiting for transfers between devices: 121 us -> 0 us
  Pallas kernels: 117 us -> 235 us
  between operations: 14.2 us -> 0.7 us
  local copies, waits for them, and re-layouts: 14 us -> 2.48 us
  starting transfers between devices: 10.2 us -> 0 us
  matrix products: 7.48 us -> 0 us
    pallas_call x0 -> x1, Pallas kernels: none -> 121 us  [route_call(): pl.pallas_call(functools.partial(route_kernel, atoms), out_shape=jax.Shap...]
    all_to_all x2 -> x0, waiting for transfers between devices: 90.2 us -> none  [the longest x1 90.2 us: per_device(): lax.all_to_all(outgoing, 'atom', split_axis=0, concat_axis=0, tiled=True)]
    all_gather x1 -> x0, waiting for transfers between devices: 29.8 us -> none  [per_device(): whole_orbitals = lax.all_gather(coefficients, 'atom', axis=0, tiled=True)]
    all_to_all x2 -> x0, starting transfers between devices: 10.2 us -> none  [the longest x1 5.53 us: per_device(): lax.all_to_all(sub_codes, 'atom', split_axis=0, concat_axis=0, tiled=True)]
    dot_general x4 -> x0, matrix products: 7.48 us -> none  [the longest x1 3.43 us: per_device(): jnp.einsum('tpmn,tni->tpmi', masked, orbital_blocks, preferred_element_ty...]
    all_to_all x2 -> x0, local copies, waits for them, and re-layouts: 7.19 us -> none  [the longest x1 6.5 us: per_device(): lax.all_to_all(outgoing, 'atom', split_axis=0, concat_axis=0, tiled=True)]
    pallas_call x1, Pallas kernels: 117 us -> 114 us  [exchange_call(): pl.pallas_call(functools.partial(exchange_kernel, atoms, auxes), out_shap...]
  transfers between devices with their start and end apart: 3 -> 0, of which waited for: 2 -> 0; matrix products, arithmetic and copies ran while one was open for 6% -> 0% of each run, Pallas kernels for 0% -> 0%
where the time goes in v2:
time: 248 us; the launch traced here: 247 us
  Pallas kernels  235 us (95%)
  other arithmetic  8.97 us (4%)
  local copies, waits for them, and re-layouts  2.48 us (1%)
    pallas_call x1, Pallas kernels, route_call(): pl.pallas_call(functools.partial(route_kernel, atoms), out_shape=jax.Shap...  121 us
    pallas_call x1, Pallas kernels, exchange_call(): pl.pallas_call(functools.partial(exchange_kernel, atoms, auxes), out_shap...  114 us

profile of v2, /device:TPU:5, one launch (start us, length us, event | category | flops | bytes accessed | tf_op | source)
XLA Modules:
  0.0 246.9 jit_solution(15679902467884229479)
XLA Ops:
  0.7 1.3 convert_element_type.26.fit_ref
  1.9 0.7 fusion
  2.7 0.8 select_reduce_fusion.3
  3.5 0.7 compare_select_fusion
  4.2 1.3 select_reduce_fusion
  5.6 0.1 eq.51
  5.6 0.1 compare_convert_fusion
  5.7 0.8 convert_element_type.22
  6.5 0.1 copy.12
  6.6 0.2 broadcast_in_dim.10
  6.8 0.2 convert_element_type.23
  7.0 0.8 broadcast_in_dim.13.code_ref
  7.8 0.1 broadcast_in_dim.11
  7.9 1.0 copy.13.mask_ref
  8.9 121.0 %shard_map.82.h_ref = bf16[8,512,128]{2,1,0:T(8,128)(2,1)} custom-call(s32[16]{0:T(128)} %get-tuple-element.7.order_ref, s32[16]{0:T(128)} %get-tuple-element.6.nu_ref, bf16[16,8,128,128]{3,2,1,0:T(8,128)(2,1)} %three_ref.1, bf16[16,128,128]{2,1,0:T(8,128)(2,1)} %copy.13.mask_ref, f32[8,2,4,8,128]{4,3,2,1,0:T(8,128)} %broadcast_in_dim.13.code_ref, ...), custom_call_target="tpu_custom_call" | custom-call | tf_op jit(solution)/shard_map/pallas_call | solution.py:464
  129.9 113.7 %shard_map.83 = f32[512,1024]{1,0:T(8,128)} custom-call(bf16[8,512,128]{2,1,0:T(8,128)(2,1)} %shard_map.82.h_ref, f32[8,32]{1,0:T(8,128)} %convert_element_type.26.fit_ref), custom_call_target="tpu_custom_call" | custom-call | tf_op jit(solution)/shard_map/pallas_call | solution.py:240
  243.7 3.2 %broadcast_multiply_fusion = f32[512,1024]{1,0:T(8,128)} fusion(f32[512,1024]{1,0:T(8,128)} %shard_map.83), kind=kLoop, calls=%fused_computation | loop fusion | flops 524288 | bytes 4194304 | tf_op jit(solution)/shard_map/mul | solution.py:523
  (2 shorter events, 0.0 us)

commit v3 on v2

--- a/solution.py
+++ b/solution.py
@@ -272,8 +272,8 @@
 
 def route_kernel(
     atoms, order_ref, nu_ref, three_ref, mask_ref, code_ref, own_ref, out_ref,
-    orbitals, outgoing, arrived, codes, acc,
-    local_sem, sx, sz0, sz, rh, sd, rd, sk, rk,
+    orbitals, outgoing, arrived, codes, acc, summed, landed,
+    local_sem, sx, sz0, sz, rh, sd, rd, sk, rk, cross_sem,
 ):
     planes, middle = atoms // 2, atoms // 2
     cap = code_ref.shape[1]
@@ -367,29 +367,36 @@
         return value.reshape(aux_here, size, occ).astype(jnp.bfloat16)
 
     def target_of(j):
-        far = (1 - side) * middle + (pos + j) % middle
-        near = side * middle + (pos + j + 1) % middle
-        return jnp.where(j < middle, far, near)
-
-    @pl.loop(0, atoms - 1)
-    def _(j):
-        target = target_of(j)
-
+        return (pos + j % (middle - 1) + 1) % middle
+
+    def start_sends(first, owner_side):
+        @pl.loop(first, first + middle - 1)
+        def _(j):
+            q = target_of(j)
+            owner = owner_side * middle + q
+            lane = (first // (middle - 1)) * middle + pos
+
+            @pl.loop(0, cap)
+            def _(r):
+                outgoing[j, r] = half_block(owner * cap + r)
+
+            device = at_atom(side * middle + q)
+            remote(outgoing.at[j], arrived.at[lane], sd.at[j], rd.at[lane], device).start()
+            remote(code_ref.at[owner], codes.at[lane], sk.at[j], rk.at[lane], device).start()
+
+    def fill_own(lane, owner, sem):
         @pl.loop(0, cap)
         def _(r):
-            outgoing[j, r] = half_block(target * cap + r)
-
-        remote(outgoing.at[j], arrived.at[me], sd.at[j], rd.at[me], at_atom(target)).start()
-        remote(code_ref.at[target], codes.at[me], sk.at[j], rk.at[me], at_atom(target)).start()
-
-    @pl.loop(0, cap)
-    def _(r):
-        arrived[me, r] = half_block(me * cap + r)
-
-    keep = pltpu.make_async_copy(code_ref.at[me], codes.at[me], local_sem.at[1])
-    keep.start()
-    keep.wait()
-    acc[...] = jnp.zeros_like(acc)
+            arrived[lane, r] = half_block(owner * cap + r)
+
+        keep = pltpu.make_async_copy(code_ref.at[owner], codes.at[lane], sem)
+        keep.start()
+        keep.wait()
+
+    start_sends(0, 1 - side)
+    fill_own(pos, (1 - side) * middle + pos, local_sem.at[1])
+    start_sends(middle - 1, side)
+    fill_own(middle + pos, me, local_sem.at[2])
 
     def take(src):
         hits = [
@@ -412,18 +419,28 @@
                     total = total + values[r] * hits[b][r][None]
                 acc[p, to, :] = total.reshape(64, occ)
 
-    take(me)
-
-    @pl.loop(0, atoms - 1)
-    def _(j):
-        near = side * middle + (pos + j + 1) % middle
-        far = (1 - side) * middle + (pos + 2 * middle - 1 - j) % middle
-        src = jnp.where(j < middle - 1, near, far)
-        remote(outgoing.at[0], arrived.at[src], sd.at[0], rd.at[src], at_atom(src)).wait_recv()
-        remote(code_ref.at[0], codes.at[src], sk.at[0], rk.at[src], at_atom(src)).wait_recv()
-        take(src)
-
-    out_ref[...] = acc[...].astype(jnp.bfloat16)
+    def take_all(base):
+        acc[...] = jnp.zeros_like(acc)
+        take(base + pos)
+
+        @pl.loop(1, middle)
+        def _(i):
+            src = (pos + middle - i) % middle
+            lane = base + src
+            device = at_atom(side * middle + src)
+            remote(outgoing.at[0], arrived.at[lane], sd.at[0], rd.at[lane], device).wait_recv()
+            remote(code_ref.at[0], codes.at[lane], sk.at[0], rk.at[lane], device).wait_recv()
+            take(lane)
+
+    across = at_atom((1 - side) * middle + pos)
+    take_all(0)
+    summed[...] = acc[...].astype(jnp.bfloat16)
+    cross = remote(summed, landed, cross_sem.at[0], cross_sem.at[1], across)
+    cross.start()
+    take_all(middle)
+    cross.wait_recv()
+    out_ref[...] = (acc[...] + landed[...].astype(jnp.float32)).astype(jnp.bfloat16)
+    cross.wait_send()
 
     @pl.when(left_ok)
     def _():
@@ -445,11 +462,11 @@
             def _():
                 along(me, own_ref, sz.at[k], -(1 - 2 * (k % 2))).wait_send()
 
-    @pl.loop(0, atoms - 1)
+    @pl.loop(0, 2 * middle - 2)
     def _(j):
-        target = target_of(j)
-        remote(outgoing.at[j], arrived.at[me], sd.at[j], rd.at[me], at_atom(target)).wait_send()
-        remote(code_ref.at[target], codes.at[me], sk.at[j], rk.at[me], at_atom(target)).wait_send()
+        device = at_atom(side * middle + target_of(j))
+        remote(outgoing.at[j], arrived.at[0], sd.at[j], rd.at[0], device).wait_send()
+        remote(code_ref.at[0], codes.at[0], sk.at[j], rk.at[0], device).wait_send()
 
 
 def route_call(order, nu, three_index, mask, codes, coefficients):
@@ -468,19 +485,22 @@
         out_specs=vmem,
         scratch_shapes=[
             pltpu.VMEM((atoms * per, size, occ), jnp.bfloat16),
-            pltpu.VMEM((atoms - 1, CAP, aux_here, size, occ), jnp.bfloat16),
+            pltpu.VMEM((atoms - 2, CAP, aux_here, size, occ), jnp.bfloat16),
             pltpu.VMEM((atoms, CAP, aux_here, size, occ), jnp.bfloat16),
             pltpu.VMEM((atoms, CAP, per, 8, 128), jnp.float32),
             pltpu.VMEM((aux_here, rows, occ), jnp.float32),
-            dma((2,)),
+            pltpu.VMEM((aux_here, rows, occ), jnp.bfloat16),
+            pltpu.VMEM((aux_here, rows, occ), jnp.bfloat16),
+            dma((3,)),
             dma((2 * planes - 1,)),
             dma((2,)),
             dma((2 * planes - 1,)),
             dma((atoms,)),
-            dma((atoms - 1,)),
+            dma((atoms - 2,)),
             dma((atoms,)),
-            dma((atoms - 1,)),
+            dma((atoms - 2,)),
             dma((atoms,)),
+            dma((2,)),
         ],
         compiler_params=pltpu.CompilerParams(
             collective_id=1, has_side_effects=True, vmem_limit_bytes=60 * 1024 * 1024

time: 248 us -> 228 us (0.919)
  Pallas kernels: 235 us -> 215 us
    pallas_call x1, Pallas kernels: 121 us -> 81.8 us  [route_call(): pl.pallas_call(functools.partial(route_kernel, atoms), out_shape=jax.Shap...]
    pallas_call x1, Pallas kernels: 114 us -> 134 us  [exchange_call(): pl.pallas_call(functools.partial(exchange_kernel, atoms, auxes), out_shap...]
where the time goes in v3:
time: 228 us
  Pallas kernels  215 us (94%)
  other arithmetic  8.97 us (4%)
  local copies, waits for them, and re-layouts  2.48 us (1%)
    pallas_call x1, Pallas kernels, exchange_call(): pl.pallas_call(functools.partial(exchange_kernel, atoms, auxes), out_shap...  134 us
    pallas_call x1, Pallas kernels, route_call(): pl.pallas_call(functools.partial(route_kernel, atoms), out_shape=jax.Shap...  81.8 us

profile of v3, /device:TPU:5, one launch (start us, length us, event | category | flops | bytes accessed | tf_op | source)
XLA Modules:
  0.0 227.6 jit_solution(1877674350451593606)
XLA Ops:
  0.7 1.3 convert_element_type.26.fit_ref
  1.9 0.7 fusion
  2.7 0.8 select_reduce_fusion.3
  3.5 0.7 compare_select_fusion
  4.2 1.3 select_reduce_fusion
  5.6 0.1 eq.51
  5.6 0.1 compare_convert_fusion
  5.7 0.8 convert_element_type.22
  6.5 0.1 copy.12
  6.6 0.2 broadcast_in_dim.10
  6.8 0.2 convert_element_type.23
  7.0 0.8 broadcast_in_dim.13.code_ref
  7.8 0.1 broadcast_in_dim.11
  7.9 1.0 copy.13.mask_ref
  8.9 81.8 %shard_map.82.h_ref = bf16[8,512,128]{2,1,0:T(8,128)(2,1)} custom-call(s32[16]{0:T(128)} %get-tuple-element.7.order_ref, s32[16]{0:T(128)} %get-tuple-element.6.nu_ref, bf16[16,8,128,128]{3,2,1,0:T(8,128)(2,1)} %three_ref.1, bf16[16,128,128]{2,1,0:T(8,128)(2,1)} %copy.13.mask_ref, f32[8,2,4,8,128]{4,3,2,1,0:T(8,128)} %broadcast_in_dim.13.code_ref, ...), custom_call_target="tpu_custom_call" | custom-call | tf_op jit(solution)/shard_map/pallas_call | solution.py:481
  90.8 133.6 %shard_map.83 = f32[512,1024]{1,0:T(8,128)} custom-call(bf16[8,512,128]{2,1,0:T(8,128)(2,1)} %shard_map.82.h_ref, f32[8,32]{1,0:T(8,128)} %convert_element_type.26.fit_ref), custom_call_target="tpu_custom_call" | custom-call | tf_op jit(solution)/shard_map/pallas_call | solution.py:240
  224.4 3.2 %broadcast_multiply_fusion = f32[512,1024]{1,0:T(8,128)} fusion(f32[512,1024]{1,0:T(8,128)} %shard_map.83), kind=kLoop, calls=%fused_computation | loop fusion | flops 524288 | bytes 4194304 | tf_op jit(solution)/shard_map/mul | solution.py:543
  (2 shorter events, 0.0 us)

commit v4 on v3

--- a/solution.py
+++ b/solution.py
@@ -279,6 +279,7 @@
     cap = code_ref.shape[1]
     per, size, occ = own_ref.shape
     aux_here = three_ref.shape[1]
+    share = aux_here // 2
     me = lax.axis_index("atom")
     ax = lax.axis_index("aux")
     hi, lo = me // 2, me % 2
@@ -357,19 +358,24 @@
 
     own.wait()
 
-    def half_block(place):
+    def half_block(place, part):
         slot, nu = order_ref[place], nu_ref[place]
         right = orbitals[nu]
-        left = three_ref[slot] * mask_ref[slot][None, :, :]
+        left = three_ref[slot, part * share:(part + 1) * share] * mask_ref[slot][None, :, :]
         value = jnp.dot(
-            left.reshape(aux_here * size, size), right, preferred_element_type=jnp.float32
+            left.reshape(share * size, size), right, preferred_element_type=jnp.float32
         )
-        return value.reshape(aux_here, size, occ).astype(jnp.bfloat16)
+        return value.reshape(share, size, occ).astype(jnp.bfloat16)
 
     def target_of(j):
         return (pos + j % (middle - 1) + 1) % middle
 
-    def start_sends(first, owner_side):
+    def block(part, j, lane, device):
+        return remote(
+            outgoing.at[part, j], arrived.at[part, lane], sd.at[part, j], rd.at[part, lane], device
+        )
+
+    def start_sends(first, owner_side, part):
         @pl.loop(first, first + middle - 1)
         def _(j):
             q = target_of(j)
@@ -378,69 +384,85 @@
 
             @pl.loop(0, cap)
             def _(r):
-                outgoing[j, r] = half_block(owner * cap + r)
+                outgoing[part, j, r] = half_block(owner * cap + r, part)
 
             device = at_atom(side * middle + q)
-            remote(outgoing.at[j], arrived.at[lane], sd.at[j], rd.at[lane], device).start()
-            remote(code_ref.at[owner], codes.at[lane], sk.at[j], rk.at[lane], device).start()
+            if part == 0:
+                remote(code_ref.at[owner], codes.at[lane], sk.at[j], rk.at[lane], device).start()
+            block(part, j, lane, device).start()
 
     def fill_own(lane, owner, sem):
         @pl.loop(0, cap)
         def _(r):
-            arrived[lane, r] = half_block(owner * cap + r)
+            for part in range(2):
+                arrived[part, lane, r] = half_block(owner * cap + r, part)
 
         keep = pltpu.make_async_copy(code_ref.at[owner], codes.at[lane], sem)
         keep.start()
         keep.wait()
 
-    start_sends(0, 1 - side)
+    start_sends(0, 1 - side, 0)
+    start_sends(0, 1 - side, 1)
     fill_own(pos, (1 - side) * middle + pos, local_sem.at[1])
-    start_sends(middle - 1, side)
+    start_sends(middle - 1, side, 0)
+    start_sends(middle - 1, side, 1)
     fill_own(middle + pos, me, local_sem.at[2])
 
-    def take(src):
+    def take(src, part):
         hits = [
             [codes[src, r, b] for r in range(cap)]
             for b in range(per)
         ]
 
-        @pl.loop(0, aux_here * (size // 64))
+        @pl.loop(0, share * (size // 64))
         def _(n):
-            p, part = n // (size // 64), n % (size // 64)
-            at = pl.ds(pl.multiple_of(part * 64, 64), 64)
+            p, row = n // (size // 64), n % (size // 64)
+            at = pl.ds(pl.multiple_of(row * 64, 64), 64)
             values = [
-                arrived[src, r, p, at, :].astype(jnp.float32).reshape(8, 8, occ)
+                arrived[part, src, r, p, at, :].astype(jnp.float32).reshape(8, 8, occ)
                 for r in range(cap)
             ]
             for b in range(per):
-                to = pl.ds(pl.multiple_of(b * size + part * 64, 64), 64)
-                total = acc[p, to, :].reshape(8, 8, occ)
+                to = pl.ds(pl.multiple_of(b * size + row * 64, 64), 64)
+                total = acc[part * share + p, to, :].reshape(8, 8, occ)
                 for r in range(cap):
                     total = total + values[r] * hits[b][r][None]
-                acc[p, to, :] = total.reshape(64, occ)
-
-    def take_all(base):
-        acc[...] = jnp.zeros_like(acc)
-        take(base + pos)
+                acc[part * share + p, to, :] = total.reshape(64, occ)
+
+    def take_all(base, part):
+        span = pl.ds(part * share, share)
+        acc[span] = jnp.zeros((share,) + acc.shape[1:], jnp.float32)
+        take(base + pos, part)
 
         @pl.loop(1, middle)
         def _(i):
             src = (pos + middle - i) % middle
             lane = base + src
             device = at_atom(side * middle + src)
-            remote(outgoing.at[0], arrived.at[lane], sd.at[0], rd.at[lane], device).wait_recv()
-            remote(code_ref.at[0], codes.at[lane], sk.at[0], rk.at[lane], device).wait_recv()
-            take(lane)
+            if part == 0:
+                remote(code_ref.at[0], codes.at[lane], sk.at[0], rk.at[lane], device).wait_recv()
+            block(part, 0, lane, device).wait_recv()
+            take(lane, part)
 
     across = at_atom((1 - side) * middle + pos)
-    take_all(0)
-    summed[...] = acc[...].astype(jnp.bfloat16)
-    cross = remote(summed, landed, cross_sem.at[0], cross_sem.at[1], across)
-    cross.start()
-    take_all(middle)
-    cross.wait_recv()
-    out_ref[...] = (acc[...] + landed[...].astype(jnp.float32)).astype(jnp.bfloat16)
-    cross.wait_send()
+    crossings = []
+    for part in range(2):
+        take_all(0, part)
+        span = pl.ds(part * share, share)
+        summed[span] = acc[span].astype(jnp.bfloat16)
+        cross = remote(
+            summed.at[span], landed.at[span], cross_sem.at[part], cross_sem.at[2 + part], across
+        )
+        cross.start()
+        crossings.append(cross)
+    take_all(middle, 0)
+    take_all(middle, 1)
+    for part in range(2):
+        crossings[part].wait_recv()
+        span = pl.ds(part * share, share)
+        out_ref[span] = (acc[span] + landed[span].astype(jnp.float32)).astype(jnp.bfloat16)
+    for cross in crossings:
+        cross.wait_send()
 
     @pl.when(left_ok)
     def _():
@@ -465,7 +487,8 @@
     @pl.loop(0, 2 * middle - 2)
     def _(j):
         device = at_atom(side * middle + target_of(j))
-        remote(outgoing.at[j], arrived.at[0], sd.at[j], rd.at[0], device).wait_send()
+        block(0, j, 0, device).wait_send()
+        block(1, j, 0, device).wait_send()
         remote(code_ref.at[0], codes.at[0], sk.at[j], rk.at[0], device).wait_send()
 
 
@@ -485,8 +508,8 @@
         out_specs=vmem,
         scratch_shapes=[
             pltpu.VMEM((atoms * per, size, occ), jnp.bfloat16),
-            pltpu.VMEM((atoms - 2, CAP, aux_here, size, occ), jnp.bfloat16),
-            pltpu.VMEM((atoms, CAP, aux_here, size, occ), jnp.bfloat16),
+            pltpu.VMEM((2, atoms - 2, CAP, aux_here // 2, size, occ), jnp.bfloat16),
+            pltpu.VMEM((2, atoms, CAP, aux_here // 2, size, occ), jnp.bfloat16),
             pltpu.VMEM((atoms, CAP, per, 8, 128), jnp.float32),
             pltpu.VMEM((aux_here, rows, occ), jnp.float32),
             pltpu.VMEM((aux_here, rows, occ), jnp.bfloat16),
@@ -496,11 +519,11 @@
             dma((2,)),
             dma((2 * planes - 1,)),
             dma((atoms,)),
+            dma((2, atoms - 2)),
+            dma((2, atoms)),
             dma((atoms - 2,)),
             dma((atoms,)),
-            dma((atoms - 2,)),
-            dma((atoms,)),
-            dma((2,)),
+            dma((4,)),
         ],
         compiler_params=pltpu.CompilerParams(
             collective_id=1, has_side_effects=True, vmem_limit_bytes=60 * 1024 * 1024

time: 228 us -> 221 us (0.969)
  Pallas kernels: 215 us -> 209 us
    pallas_call x1, Pallas kernels: 134 us -> 122 us  [exchange_call(): pl.pallas_call(functools.partial(exchange_kernel, atoms, auxes), out_shap...]
    pallas_call x1, Pallas kernels: 81.8 us -> 87 us  [route_call(): pl.pallas_call(functools.partial(route_kernel, atoms), out_shape=jax.Shap...]
where the time goes in v4:
time: 221 us
  Pallas kernels  209 us (95%)
  other arithmetic  8.97 us (4%)
  local copies, waits for them, and re-layouts  2.48 us (1%)
    pallas_call x1, Pallas kernels, exchange_call(): pl.pallas_call(functools.partial(exchange_kernel, atoms, auxes), out_shap...  122 us
    pallas_call x1, Pallas kernels, route_call(): pl.pallas_call(functools.partial(route_kernel, atoms), out_shape=jax.Shap...  87 us

profile of v4, /device:TPU:5, one launch (start us, length us, event | category | flops | bytes accessed | tf_op | source)
XLA Modules:
  0.0 221.1 jit_solution(6628303083012027195)
XLA Ops:
  0.7 1.3 convert_element_type.26.fit_ref
  1.9 0.7 fusion
  2.7 0.8 select_reduce_fusion.3
  3.5 0.7 compare_select_fusion
  4.2 1.3 select_reduce_fusion
  5.6 0.1 eq.51
  5.6 0.1 compare_convert_fusion
  5.7 0.8 convert_element_type.22
  6.5 0.1 copy.12
  6.6 0.2 broadcast_in_dim.10
  6.8 0.2 convert_element_type.23
  7.0 0.8 broadcast_in_dim.13.code_ref
  7.8 0.1 broadcast_in_dim.11
  7.9 1.0 copy.13.mask_ref
  8.9 87.0 %shard_map.82.h_ref = bf16[8,512,128]{2,1,0:T(8,128)(2,1)} custom-call(s32[16]{0:T(128)} %get-tuple-element.7.order_ref, s32[16]{0:T(128)} %get-tuple-element.6.nu_ref, bf16[16,8,128,128]{3,2,1,0:T(8,128)(2,1)} %three_ref.1, bf16[16,128,128]{2,1,0:T(8,128)(2,1)} %copy.13.mask_ref, f32[8,2,4,8,128]{4,3,2,1,0:T(8,128)} %broadcast_in_dim.13.code_ref, ...), custom_call_target="tpu_custom_call" | custom-call | tf_op jit(solution)/shard_map/pallas_call | solution.py:504
  95.9 122.0 %shard_map.83 = f32[512,1024]{1,0:T(8,128)} custom-call(bf16[8,512,128]{2,1,0:T(8,128)(2,1)} %shard_map.82.h_ref, f32[8,32]{1,0:T(8,128)} %convert_element_type.26.fit_ref), custom_call_target="tpu_custom_call" | custom-call | tf_op jit(solution)/shard_map/pallas_call | solution.py:240
  217.9 3.2 %broadcast_multiply_fusion = f32[512,1024]{1,0:T(8,128)} fusion(f32[512,1024]{1,0:T(8,128)} %shard_map.83), kind=kLoop, calls=%fused_computation | loop fusion | flops 524288 | bytes 4194304 | tf_op jit(solution)/shard_map/mul | solution.py:566
  (2 shorter events, 0.0 us)

commit v5 on v4

--- a/solution.py
+++ b/solution.py
@@ -406,7 +406,6 @@
     fill_own(pos, (1 - side) * middle + pos, local_sem.at[1])
     start_sends(middle - 1, side, 0)
     start_sends(middle - 1, side, 1)
-    fill_own(middle + pos, me, local_sem.at[2])
 
     def take(src, part):
         hits = [
@@ -455,6 +454,7 @@
         )
         cross.start()
         crossings.append(cross)
+    fill_own(middle + pos, me, local_sem.at[2])
     take_all(middle, 0)
     take_all(middle, 1)
     for part in range(2):

time: 221 us -> 221 us (level)
  no operation moved by 1% of the time
where the time goes in v5:
time: 221 us
  Pallas kernels  209 us (95%)
  other arithmetic  8.97 us (4%)
  local copies, waits for them, and re-layouts  2.48 us (1%)
    pallas_call x1, Pallas kernels, exchange_call(): pl.pallas_call(functools.partial(exchange_kernel, atoms, auxes), out_shap...  122 us
    pallas_call x1, Pallas kernels, route_call(): pl.pallas_call(functools.partial(route_kernel, atoms), out_shape=jax.Shap...  87 us

profile of v5, /device:TPU:5, one launch (start us, length us, event | category | flops | bytes accessed | tf_op | source)
XLA Modules:
  0.0 221.1 jit_solution(5371387689038790810)
XLA Ops:
  0.7 1.3 convert_element_type.26.fit_ref
  1.9 0.7 fusion
  2.7 0.8 select_reduce_fusion.3
  3.5 0.7 compare_select_fusion
  4.2 1.3 select_reduce_fusion
  5.6 0.1 eq.51
  5.6 0.1 compare_convert_fusion
  5.7 0.8 convert_element_type.22
  6.5 0.1 copy.12
  6.6 0.2 broadcast_in_dim.10
  6.8 0.2 convert_element_type.23
  7.0 0.8 broadcast_in_dim.13.code_ref
  7.8 0.1 broadcast_in_dim.11
  7.9 1.0 copy.13.mask_ref
  8.9 87.0 %shard_map.82.h_ref = bf16[8,512,128]{2,1,0:T(8,128)(2,1)} custom-call(s32[16]{0:T(128)} %get-tuple-element.7.order_ref, s32[16]{0:T(128)} %get-tuple-element.6.nu_ref, bf16[16,8,128,128]{3,2,1,0:T(8,128)(2,1)} %three_ref.1, bf16[16,128,128]{2,1,0:T(8,128)(2,1)} %copy.13.mask_ref, f32[8,2,4,8,128]{4,3,2,1,0:T(8,128)} %broadcast_in_dim.13.code_ref, ...), custom_call_target="tpu_custom_call" | custom-call | tf_op jit(solution)/shard_map/pallas_call | solution.py:504
  95.9 122.0 %shard_map.83 = f32[512,1024]{1,0:T(8,128)} custom-call(bf16[8,512,128]{2,1,0:T(8,128)(2,1)} %shard_map.82.h_ref, f32[8,32]{1,0:T(8,128)} %convert_element_type.26.fit_ref), custom_call_target="tpu_custom_call" | custom-call | tf_op jit(solution)/shard_map/pallas_call | solution.py:240
  217.9 3.2 %broadcast_multiply_fusion = f32[512,1024]{1,0:T(8,128)} fusion(f32[512,1024]{1,0:T(8,128)} %shard_map.83), kind=kLoop, calls=%fused_computation | loop fusion | flops 524288 | bytes 4194304 | tf_op jit(solution)/shard_map/mul | solution.py:566
  (2 shorter events, 0.0 us)
